TPU v7x, 128 devices: a whole 4x4x4 slice. The times are simulated.
128 devices in a mesh: row: 16 (over x, y_lo, core), col: 8 (over y_hi, z).
Axes of the slice: x: 4, y: 4 (y_hi: 2, y_lo: 2; y = y_hi * 2 + y_lo), z: 4, core: 2. Of those that a mesh axis runs over, the one named last changes fastest.
Arguments:
- hidden_states: bfloat16 [16384, 2048], P('row', 'col'), may hold values from -21 to 21
- lengths: int32 [32], P('row'), may hold values from 16 to 512, as said below
- qkvg_master: float32 [2048, 12288], P(('row', 'col')), may hold values from -0.125 to 0.125
- gateup_master: float32 [2, 2048, 4096], P(None, ('row', 'col')), may hold values from -0.125 to 0.125
- out_master: float32 [4096, 2048], P(None, ('row', 'col')), may hold values from -0.09375 to 0.09375
- down_master: float32 [4096, 2048], P(None, ('row', 'col')), may hold values from -0.09375 to 0.09375
Outputs:
- layer_output: bfloat16 [16384, 2048], P('row', 'col')
- qkvg_weight: bfloat16 [2048, 12288], P('row', 'col')
- gateup_weight: bfloat16 [2, 2048, 4096], P(None, 'row', 'col')
- mixing_weight: bfloat16 [4096, 2048], P('col', 'row')
- down_weight: bfloat16 [4096, 2048], P('col', 'row')
Inputs may be any that keep to these rules, and one draw needn't show every extreme that they name: `lengths`: prompt length of each request; the positions of a request from its length on are padding. Some request has length 512 in every draw.
All inputs are finite; a program needn't handle non-finite values.
Results may differ from a plain program's by a relative error of at most 0.014.
Values may be sent and summed in bfloat16 or wider, within the bound.
A program may use at most 128 MiB of HBM per device.

v0:
```python
import math
import jax
import jax.numpy as jnp
from jax import lax
from jax.sharding import PartitionSpec as P

D = 2048
HEADS = 8
KEY = 256
VAL = 512
S = 512
BLOCK = 256
epsilon = 1e-05


def rms_round(values):
    scale = lax.rsqrt(jnp.mean(values * values, axis=-1, keepdims=True) + epsilon)
    return (values * scale).astype(jnp.bfloat16)


def rotate(values, positions):
    half = values.shape[-1] // 2
    freq = jnp.power(10000.0, -2.0 * jnp.arange(half).astype(jnp.float32) / values.shape[-1])
    angle = positions.astype(jnp.float32)[:, None] * freq[None, :]
    cosine = jnp.cos(angle)[:, None, :]
    sine = jnp.sin(angle)[:, None, :]
    first = values[..., :half]
    second = values[..., half:]
    return jnp.concatenate(
        [first * cosine - second * sine, first * sine + second * cosine], axis=-1
    )


def retain(gammas, query, keyed, value):
    heads = query.shape[1]
    blocks = S // BLOCK
    offsets = jnp.arange(BLOCK)
    lag = offsets[:, None] - offsets[None, :]
    within = jnp.where(
        (lag >= 0)[None],
        jnp.power(gammas[:, None, None], jnp.maximum(lag, 0).astype(jnp.float32)[None]),
        0.0,
    )
    into = jnp.power(gammas[:, None], (offsets + 1).astype(jnp.float32)[None, :])
    leaving = jnp.power(gammas[:, None], (BLOCK - 1 - offsets).astype(jnp.float32)[None, :])
    across_blocks_sum = jnp.power(gammas, 1.0 * BLOCK)
    upper_bound = lax.Precision.HIGHEST

    def advance(carry, inputs):
        retention_state, key_sum = carry
        query_block, key_block, value_tile_rows = inputs
        scores = (
            jnp.einsum("thk,shk->hts", query_block, key_block, preferred_element_type=jnp.float32)
            * within
        )
        denom_inside = jnp.sum(scores, axis=2)
        inside = jnp.einsum(
            "hts,shv->thv",
            scores.astype(jnp.bfloat16),
            value_tile_rows,
            preferred_element_type=jnp.float32,
        )
        damped_query_rows = query_block.astype(jnp.float32) * jnp.transpose(into)[:, :, None]
        carried_state = jnp.einsum(
            "swc,wcm->swm", damped_query_rows, retention_state, precision=upper_bound
        )
        denom_carried = jnp.einsum("thk,hk->th", damped_query_rows, key_sum, precision=upper_bound)
        damped_key_rows = key_block.astype(jnp.float32) * jnp.transpose(leaving)[:, :, None]
        retention_state = across_blocks_sum[:, None, None] * retention_state + jnp.einsum(
            "wat,wag->atg",
            damped_key_rows,
            value_tile_rows.astype(jnp.float32),
            precision=upper_bound,
        )
        key_sum = across_blocks_sum[:, None] * key_sum + jnp.sum(damped_key_rows, axis=0)
        denom = jnp.transpose(denom_inside) + denom_carried
        result = (inside + carried_state) / jnp.maximum(jnp.abs(denom), 1.0)[:, :, None]
        return ((retention_state, key_sum), result)

    start = (jnp.zeros((heads, KEY, VAL), jnp.float32), jnp.zeros((heads, KEY), jnp.float32))
    sliced = (
        query.reshape(blocks, BLOCK, heads, KEY),
        keyed.reshape(blocks, BLOCK, heads, KEY),
        value.reshape(blocks, BLOCK, heads, VAL),
    )
    _, results = lax.scan(advance, start, sliced)
    return results.reshape(S, heads, VAL)


def gate_heads(retained, gate):
    centre = jnp.mean(retained, axis=-1, keepdims=True)
    centred = retained - centre
    spread = jnp.mean(centred * centred, axis=-1, keepdims=True)
    grouped = centred * lax.rsqrt(spread + epsilon)
    return (jax.nn.silu(gate.astype(jnp.float32)) * grouped).astype(jnp.bfloat16)


def shards(hidden_states, lengths, qkvg_master, gateup_master, out_master, down_master):
    tok_rows = hidden_states.shape[0]
    share_width = hidden_states.shape[1]
    requests = lengths.shape[0]
    head_count = HEADS // lax.axis_size("col")
    head_width = 2 * KEY + 2 * VAL
    in_blocks = (
        lax.all_to_all(
            qkvg_master.astype(jnp.bfloat16)[None], "col", split_axis=2, concat_axis=1, tiled=True
        ),
        lax.all_to_all(
            gateup_master.astype(jnp.bfloat16), "col", split_axis=2, concat_axis=1, tiled=True
        ),
    )
    qkvg_blocks = in_blocks[0][0]
    gateup_blocks = in_blocks[1]
    out_blocks, down_blocks = (
        lax.all_to_all(
            out_master.astype(jnp.bfloat16), "col", split_axis=0, concat_axis=1, tiled=True
        ),
        lax.all_to_all(
            down_master.astype(jnp.bfloat16), "col", split_axis=0, concat_axis=1, tiled=True
        ),
    )
    gathered = lax.all_gather(hidden_states, "col", axis=1, tiled=True)
    normed = rms_round(gathered.astype(jnp.float32))
    columns = normed
    projected = jnp.dot(
        columns,
        lax.all_gather(qkvg_blocks, "row", axis=0, tiled=True),
        preferred_element_type=jnp.float32,
    )
    projected = projected.astype(jnp.bfloat16).reshape(requests, S, head_count, head_width)
    positions = jnp.arange(S)
    query = rotate(projected[..., :KEY].astype(jnp.float32), positions).astype(jnp.bfloat16)
    keyed = (
        rotate(projected[..., KEY : 2 * KEY].astype(jnp.float32), positions)
        * (1.0 / math.sqrt(KEY))
    ).astype(jnp.bfloat16)
    value = projected[..., 2 * KEY : 2 * KEY + VAL]
    gate = projected[..., 2 * KEY + VAL :]
    head_ids = lax.axis_index("col") * head_count + jnp.arange(head_count)
    gammas = 1.0 - jnp.power(2.0, -5.0 - head_ids.astype(jnp.float32))
    retained = jax.vmap(retain, in_axes=(None, 0, 0, 0))(gammas, query, keyed, value)
    mixed = gate_heads(retained, gate).reshape(tok_rows, head_count * VAL)
    partial_mix = jnp.dot(
        mixed,
        lax.all_gather(out_blocks, "row", axis=1, tiled=True),
        preferred_element_type=jnp.float32,
    )
    residual = hidden_states.astype(jnp.float32) + lax.psum_scatter(
        partial_mix.astype(jnp.bfloat16), "col", scatter_dimension=1, tiled=True
    ).astype(jnp.float32)
    squares = lax.psum(jnp.sum(residual * residual, axis=1), "col")
    normed_share = (residual * lax.rsqrt(squares[:, None] / D + epsilon)).astype(jnp.bfloat16)
    normed_mid = lax.all_gather(normed_share, "col", axis=1, tiled=True)
    columns = normed_mid
    paired = jnp.einsum(
        "td,gdf->gtf",
        columns,
        lax.all_gather(gateup_blocks, "row", axis=1, tiled=True),
        preferred_element_type=jnp.float32,
    )
    hidden = (jax.nn.silu(paired[0]) * paired[1]).astype(jnp.bfloat16)
    partial_feed = jnp.dot(
        hidden,
        lax.all_gather(down_blocks, "row", axis=1, tiled=True),
        preferred_element_type=jnp.float32,
    )
    feed = lax.psum_scatter(
        partial_feed.astype(jnp.bfloat16), "col", scatter_dimension=1, tiled=True
    ).astype(jnp.float32)
    live = positions[None, :] < lengths[:, None]
    summed = (residual + feed).reshape(requests, S, share_width)
    layer_output = (
        jnp.where(live[:, :, None], summed, 0.0).astype(jnp.bfloat16).reshape(tok_rows, share_width)
    )
    return (layer_output, qkvg_blocks, gateup_blocks, out_blocks, down_blocks)


def solution(mesh):
    return jax.shard_map(
        shards,
        mesh=mesh,
        in_specs=(
            P("row", "col"),
            P("row"),
            P(("row", "col"), None),
            P(None, ("row", "col"), None),
            P(None, ("row", "col")),
            P(None, ("row", "col")),
        ),
        out_specs=(
            P("row", "col"),
            P("row", "col"),
            P(None, "row", "col"),
            P("col", "row"),
            P("col", "row"),
        ),
        check_vma=False,
    )
```

profile of v0, /device:TPU:0, one launch (start us, length us, event | category | flops | bytes accessed | tf_op | source)
XLA Modules:
  0.0 546.4 jit_solution(4470054809173031747)
XLA Ops:
  9.1 9.8 %copy.81 = bf16[1,16,12288]{1,0,2:T(2,128)(2,1)} copy(bf16[1,16,12288]{2,1,0:T(8,128)(2,1)S(1)} %convert_bitcast_fusion) | data formatting | bytes 786432 | tf_op jit(solution)/shard_map/broadcast_in_dim | solution.py:106
  19.4 67.0 %reduce.7 = bf16[12288,16]{1,0:T(8,128)(2,1)S(1)} reduce(bf16[12288,1,16]{2,1,0:T(2,128)(2,1)} %bitcast.202, bf16[]{:T(256)} %broadcast.312), dimensions={1}, to_apply=%bitcast.147.reduce_sub_computation | reduce | bytes 786434
  86.4 3.3 reshape.460
  89.7 18.0 %all_to_all.71 = bf16[8,2,12288]{2,1,0:T(2,128)(2,1)S(1)} all-to-all(bf16[8,2,12288]{2,1,0:T(2,128)(2,1)S(1)} %reshape.460), channel_id=1, replica_groups=mesh['row'=16,'col'=8] {'col'}, dimensions={0} | all-to-all | bytes 786432 | tf_op jit(solution)/shard_map/all_to_all | solution.py:105
  107.7 6.2 %reshape.461 = bf16[12288,1,16]{2,1,0:T(2,128)(2,1)} reshape(bf16[8,2,12288]{2,1,0:T(2,128)(2,1)S(1)} %all_to_all.71) | data formatting | bytes 786432
  114.0 11.4 %copy.82 = bf16[1,16,12288]{2,1,0:T(8,128)(2,1)S(1)} copy(bf16[1,16,12288]{1,0,2:T(2,128)(2,1)} %bitcast.203) | data formatting | bytes 786432 | tf_op jit(solution)/shard_map/all_to_all | solution.py:105
  127.1 3.4 all-to-all-start.1
  131.7 6.8 %all-to-all-done.1 = bf16[8,512,16]{1,2,0:T(8,128)(2,1)S(1)} async-done(((bf16[8,512,16]{1,2,0:T(8,128)(2,1)}), bf16[8,512,16]{1,2,0:T(8,128)(2,1)S(1)}, u32[]{:S(2)}, u32[]{:S(2)}) %all-to-all-start.1) | async-done | bytes 131104 | tf_op jit(solution)/shard_map/all_to_all | solution.py:115
  139.5 3.1 fusion.45
  142.6 23.4 %all-gather.9.cloned.1.call-done = bf16[2048,1536]{1,0:T(8,128)(2,1)} async-done(((bf16[128,1536]{1,0:T(8,128)(2,1)}), bf16[2048,1536]{1,0:T(8,128)(2,1)}) %all-gather.9.cloned.1.call-update) | async-done | bytes 6291472 | tf_op jit(solution)/shard_map/all_gather | solution.py:127
  166.1 10.5 %fusion.52 = bf16[1024,1536]{1,0:T(8,128)(2,1)S(1)} fusion(bf16[2048,1536]{1,0:T(8,128)(2,1)} %all-gather.9.cloned.1.call-done, bf16[1024,2048]{1,0:T(8,128)(2,1)} %all-gather.7.cloned.1.call-done, f32[1024]{0:T(1024)S(1)} %add_rsqrt_fusion.1), kind=kOutput, calls=%fused_computation.65 | convolution fusion | flops 6450315264 | bytes 13635584 | tf_op jit(solution)/shard_map/dot_general | solution.py:125
  178.6 18.9 %while.17 = (s32[]{:T(128)}, f32[2,1,256,512]{3,2,0,1:T(8,128)S(1)}, f32[2,1,256]{2,1,0:T(1,128)S(1)}, f32[2,2,256,1,512]{4,2,0,1,3:T(8,128)}, f32[1]{0:T(128)},...) while((s32[]{:T(128)}, ...), condition=%wide.region_4.5_spmd.clone.clone.clone, body=%wide.region_1.4_spmd.clone.clone.clone.sunk | while | flops 1816989184 | bytes 22576332 | solution.py:86
  185.9 2.0 fusion.98
  189.4 2.0 convolution_bitcast_fusion.3
  195.4 2.0 fusion.98
  197.5 2.0 bitcast_reduce_fusion
  200.3 2.1 fusion.67
  203.2 5.9 %convolution_convert_fusion.1 = bf16[1024,2048]{1,0:T(8,128)(2,1)} fusion(bf16[1024,512]{1,0:T(8,128)(2,1)S(1)} %bitcast.224, bf16[512,2048]{0,1:T(8,128)(2,1)} %all-gather.11.cloned.1.call-done), kind=kOutput, calls=%fused_computation.67 | convolution fusion | flops 2149580800 | bytes 7340032 | tf_op jit(solution)/shard_map/dot_general | solution.py:143
  210.2 2.7 copy.89
  213.0 2.2 reshape.458
  215.2 17.3 %all_to_all.72 = bf16[8,2,8192]{2,1,0:T(2,128)(2,1)S(1)} all-to-all(bf16[8,2,8192]{2,1,0:T(2,128)(2,1)S(1)} %reshape.458), channel_id=1, replica_groups=mesh['row'=16,'col'=8] {'col'}, dimensions={0} | all-to-all | bytes 524288 | tf_op jit(solution)/shard_map/all_to_all | solution.py:108
  233.9 3.3 copy.90
  237.2 59.2 %reduce-scatter.3.cloned.1.call-done = bf16[1024,256]{1,0:T(8,128)(2,1)} async-done(((bf16[1024,2048]{1,0:T(8,128)(2,1)}), bf16[1024,256]{1,0:T(8,128)(2,1)}) %reduce-scatter.3.cloned.1.call-update) | async-done | bytes 524304 | tf_op jit(solution)/shard_map/reduce_scatter | solution.py:148
  297.8 21.4 %psum.7 = f32[1024]{0:T(1024)S(1)} all-reduce(f32[1024]{0:T(1024)S(1)} %multiply_reduce_fusion), channel_id=1, replica_groups=mesh['row'=16,'col'=8] {'col'}, use_global_device_ids=true, to_apply=%region_9.10 | all-reduce | flops 1024 | bytes 8192 | tf_op jit(solution)/shard_map/psum | solution.py:151
  319.2 2.1 multiply_convert_fusion
  321.4 12.9 %all_to_all.73 = bf16[8,512,16]{1,2,0:T(8,128)(2,1)} all-to-all(bf16[8,512,16]{1,2,0:T(8,128)(2,1)S(1)} %bitcast.227), channel_id=1, replica_groups=mesh['row'=16,'col'=8] {'col'}, dimensions={0} | all-to-all | bytes 262144 | tf_op jit(solution)/shard_map/all_to_all | solution.py:118
  335.3 76.4 %all-gather.13.cloned.1.call-done = bf16[1024,2048]{1,0:T(8,128)(2,1)} async-done(((bf16[1024,256]{1,0:T(8,128)(2,1)}), bf16[1024,2048]{1,0:T(8,128)(2,1)}) %all-gather.13.cloned.1.call-update) | async-done | bytes 4194320 | tf_op jit(solution)/shard_map/all_gather | solution.py:153
  411.7 9.9 %fusion.55 = f32[2,1024,512]{2,1,0:T(8,128)} fusion(bf16[2,2048,512]{2,1,0:T(8,128)(2,1)} %all-gather.15.cloned.1.call-done, bf16[1024,2048]{1,0:T(8,128)(2,1)} %all-gather.13.cloned.1.call-done), kind=kOutput, calls=%fused_computation.70 | convolution fusion | flops 4294967296 | bytes 12582912 | tf_op jit(solution)/shard_map/td,gdf->gtf/dot_general | solution.py:155
  421.6 23.7 %all-gather.17.cloned.1.call-done = bf16[512,2048]{0,1:T(8,128)(2,1)} async-done(((bf16[512,128]{0,1:T(8,128)(2,1)}), bf16[512,2048]{0,1:T(8,128)(2,1)}) %all-gather.17.cloned.1.call-update) | async-done | bytes 2097168 | tf_op jit(solution)/shard_map/all_gather | solution.py:164
  445.3 7.2 %convolution_convert_fusion = bf16[1024,2048]{1,0:T(8,128)(2,1)} fusion(bf16[512,2048]{0,1:T(8,128)(2,1)} %all-gather.17.cloned.1.call-done, f32[2,1024,512]{2,1,0:T(8,128)} %fusion.55), kind=kOutput, calls=%fused_computation.66 | convolution fusion | flops 2152726528 | bytes 10485760 | tf_op jit(solution)/shard_map/dot_general | solution.py:162
  454.9 82.5 %reduce-scatter.5.cloned.1.call-done = bf16[1024,256]{1,0:T(8,128)(2,1)} async-done(((bf16[1024,2048]{1,0:T(8,128)(2,1)}), bf16[1024,256]{1,0:T(8,128)(2,1)}) %reduce-scatter.5.cloned.1.call-update) | async-done | bytes 524304 | tf_op jit(solution)/shard_map/reduce_scatter | solution.py:167
  537.4 2.1 select_convert_fusion
  (104 shorter events, 29.9 us)
Async XLA Ops:
  7.2 132.3 %all-gather.7.cloned.1.call-start = ((), (), s32[]{:S(2)}) async-start(), calls=%async_computation.6 | async-start | bytes 4718592 | tf_op jit(solution)/shard_map/all_gather | solution.py:122
  7.9 158.2 %all-gather.9.cloned.1.call-start = ((), (), s32[]{:S(2)}) async-start(), calls=%async_computation.7 | async-start | bytes 6684672 | tf_op jit(solution)/shard_map/all_gather | solution.py:127
  125.4 1.1 copy-start.10
  127.1 11.4 %all-to-all-start.1 = ((bf16[8,512,16]{1,2,0:T(8,128)(2,1)}), bf16[8,512,16]{1,2,0:T(8,128)(2,1)S(1)}, u32[]{:S(2)}, u32[]{:S(2)}) async-start(bf16[8,512,16]{1,2,0:T(8,128)(2,1)} %bitcast.160), calls=%async_computation.1 | async-start | bytes 262144 | tf_op jit(solution)/shard_map/all_to_all | solution.py:115
  130.5 72.7 %all-gather.11.cloned.1.call-start = ((), (), s32[]{:S(2)}) async-start(), calls=%async_computation.8 | async-start | bytes 2228224 | tf_op jit(solution)/shard_map/all_gather | solution.py:145
  138.5 0.7 copy-start.6
  139.2 157.3 %reduce-scatter.3.cloned.1.call-start = ((), (), s32[]{:S(2)}) async-start(), calls=%async_computation.9 | async-start | bytes 4718592 | tf_op jit(solution)/shard_map/reduce_scatter | solution.py:148
  176.6 1.7 copy-start.5
  178.6 3.3 copy-start.1
  185.9 2.1 copy-start.2
  188.1 3.3 copy-start.1
  195.4 2.2 copy-start.2
  197.5 2.3 copy-start
  209.2 1.0 copy-start.9
  209.2 126.1 %all-gather.15.cloned.1.call-start = ((), (), s32[]{:S(2)}) async-start(), calls=%async_computation.11 | async-start | bytes 4456448 | tf_op jit(solution)/shard_map/all_gather | solution.py:158
  232.5 64.0 %copy-start.3 = (bf16[1024,256]{1,0:T(8,128)(2,1)S(1)}, bf16[1024,256]{1,0:T(8,128)(2,1)}, u32[]{:S(2)}) copy-start(bf16[1024,256]{1,0:T(8,128)(2,1)} %param.8) | copy-start | bytes 1572868
  237.2 84.1 %copy-start.11 = (f32[4096,16]{0,1:T(8,128)S(1)}, f32[4096,16]{0,1:T(8,128)}, u32[]{:S(2)}) copy-start(f32[4096,16]{0,1:T(8,128)} %param.13) | copy-start | bytes 786436
  237.2 174.5 %all-gather.13.cloned.1.call-start = ((), (), s32[]{:S(2)}) async-start(), calls=%async_computation.10 | async-start | bytes 4718592 | tf_op jit(solution)/shard_map/all_gather | solution.py:153
  321.3 124.0 %all-gather.17.cloned.1.call-start = ((), (), s32[]{:S(2)}) async-start(), calls=%async_computation.12 | async-start | bytes 2228224 | tf_op jit(solution)/shard_map/all_gather | solution.py:164
  334.3 203.2 %reduce-scatter.5.cloned.1.call-start = ((), (), s32[]{:S(2)}) async-start(), calls=%async_computation.13 | async-start | bytes 4718592 | tf_op jit(solution)/shard_map/reduce_scatter | solution.py:167
  452.5 0.7 copy-start.12
  452.5 0.9 copy-start.7
  452.5 1.7 copy-start.8
  452.5 85.0 %copy-start.4 = (bf16[1024,256]{1,0:T(8,128)(2,1)S(1)}, bf16[1024,256]{1,0:T(8,128)(2,1)}, u32[]{:S(2)}) copy-start(bf16[1024,256]{1,0:T(8,128)(2,1)} %reduce-scatter.3.cloned.1.call-done) | copy-start | bytes 1572868
Sparse Core Ops, SparseCore 0:
  10.2 76.3 all-gather.6
  126.6 39.4 all-gather.8
  168.3 34.8 all-gather.10
  209.3 87.1 reduce-scatter.2
  298.7 36.6 all-gather.14
  338.2 73.4 all-gather.12
  413.5 31.7 all-gather.16
  452.6 84.7 reduce-scatter.4
where the time goes:
time: 547 us; the launch traced here: 546 us
  waiting for transfers between devices  275 us (50%)
  other arithmetic  84 us (15%)
  blocking collectives  69.6 us (13%)
  local copies, waits for them, and re-layouts  53.3 us (10%)
  matrix products  46 us (8%)
  between operations  14.5 us (3%)
    reduce_scatter x1, waiting for transfers between devices, shards(): lax.psum_scatter(partial_feed.astype(jnp.bfloat16), 'col', scatter_dimens...  82.5 us
    all_gather x1, waiting for transfers between devices, shards(): normed_mid = lax.all_gather(normed_share, 'col', axis=1, tiled=True)  76.4 us
    unnamed x5, other arithmetic  67 us
    reduce_scatter x1, waiting for transfers between devices, shards(): lax.psum_scatter(partial_mix.astype(jnp.bfloat16), 'col', scatter_dimensi...  59.2 us
    all_gather x1, waiting for transfers between devices, shards(): lax.all_gather(down_blocks, 'row', axis=1, tiled=True)  23.7 us
    all_gather x1, waiting for transfers between devices, shards(): lax.all_gather(qkvg_blocks, 'row', axis=0, tiled=True)  23.4 us
    psum x1, blocking collectives, shards(): squares = lax.psum(jnp.sum(residual * residual, axis=1), 'col')  21.4 us
    unnamed x32, local copies, waits for them, and re-layouts  19.1 us
  transfers between devices with their start and end apart: 9, of which 8 were waited for; matrix products, arithmetic and copies ran while one was open for 30% of the time, Pallas kernels for 0%

commit v1 on v0

--- a/solution.py
+++ b/solution.py
@@ -1,3 +1,4 @@
+import functools
 import math
 import jax
 import jax.numpy as jnp
@@ -11,6 +12,16 @@
 S = 512
 BLOCK = 256
 epsilon = 1e-05
+
+
+def wait_tables(xx, mesh_name):
+    item_now = lax.all_to_all(
+        jnp.stack([xx for _ in range(lax.psum(1, mesh_name))], 0), mesh_name, 0, 0
+    )
+    return jnp.concatenate(item_now, 0)
+
+
+raise_tiles_now = functools.partial(wait_tables, mesh_name="row")
 
 
 def rms_round(values):
@@ -122,11 +133,7 @@
     gathered = lax.all_gather(hidden_states, "col", axis=1, tiled=True)
     normed = rms_round(gathered.astype(jnp.float32))
     columns = normed
-    projected = jnp.dot(
-        columns,
-        lax.all_gather(qkvg_blocks, "row", axis=0, tiled=True),
-        preferred_element_type=jnp.float32,
-    )
+    projected = jnp.dot(columns, raise_tiles_now(qkvg_blocks), preferred_element_type=jnp.float32)
     projected = projected.astype(jnp.bfloat16).reshape(requests, S, head_count, head_width)
     positions = jnp.arange(S)
     query = rotate(projected[..., :KEY].astype(jnp.float32), positions).astype(jnp.bfloat16)

time: 547 us -> 623 us (1.14)
  waiting for transfers between devices: 275 us -> 351 us
  blocking collectives: 69.6 us -> 53.6 us
  starting transfers between devices: 4.1 us -> 16.8 us
    all_to_all x0 -> x2, waiting for transfers between devices: none -> 107 us  [the longest x1 97.8 us: wait_tables(): lax.all_to_all(jnp.stack([xx for _ in range(lax.psum(1, mesh_name))], 0),...]
    all_gather x1 -> x0, waiting for transfers between devices: 23.4 us -> none  [shards(): lax.all_gather(qkvg_blocks, 'row', axis=0, tiled=True)]
    all_to_all x1 -> x0, blocking collectives: 18 us -> none  [shards(): lax.all_to_all(qkvg_master.astype(jnp.bfloat16)[None], 'col', split_axis=...]
    all_to_all x0 -> x2, starting transfers between devices: none -> 12.7 us  [the longest x1 8.06 us: shards(): lax.all_to_all(qkvg_master.astype(jnp.bfloat16)[None], 'col', split_axis=...]
    all_to_all x1, waiting for transfers between devices: 6.84 us -> 0.01 us  [shards(): lax.all_to_all(out_master.astype(jnp.bfloat16), 'col', split_axis=0, conc...]
    unnamed x32 -> x34, local copies, waits for them, and re-layouts: 19.1 us -> 19.1 us
  transfers between devices with their start and end apart: 9 -> 10, of which waited for: 8 -> 7; matrix products, arithmetic and copies ran while one was open for 30% -> 27% of each run, Pallas kernels for 0% -> 0%
where the time goes in v1:
time: 623 us; the launch traced here: 622 us
  waiting for transfers between devices  351 us (56%)
  other arithmetic  83.9 us (13%)
  local copies, waits for them, and re-layouts  55.7 us (9%)
  blocking collectives  53.6 us (9%)
  matrix products  45.9 us (7%)
  starting transfers between devices  16.8 us (3%)
  between operations  14.5 us (2%)
    all_to_all x1, waiting for transfers between devices, wait_tables(): lax.all_to_all(jnp.stack([xx for _ in range(lax.psum(1, mesh_name))], 0),...  97.8 us
    reduce_scatter x1, waiting for transfers between devices, shards(): lax.psum_scatter(partial_feed.astype(jnp.bfloat16), 'col', scatter_dimens...  82.6 us
    all_gather x1, waiting for transfers between devices, shards(): normed_mid = lax.all_gather(normed_share, 'col', axis=1, tiled=True)  76.5 us
    unnamed x5, other arithmetic  67 us
    reduce_scatter x1, waiting for transfers between devices, shards(): lax.psum_scatter(partial_mix.astype(jnp.bfloat16), 'col', scatter_dimensi...  60.2 us
    all_gather x1, waiting for transfers between devices, shards(): lax.all_gather(down_blocks, 'row', axis=1, tiled=True)  23.5 us
    psum x1, blocking collectives, shards(): squares = lax.psum(jnp.sum(residual * residual, axis=1), 'col')  21.3 us
    all_to_all x1, blocking collectives, shards(): lax.all_to_all(gateup_master.astype(jnp.bfloat16), 'col', split_axis=2, c...  19.3 us
  transfers between devices with their start and end apart: 10, of which 7 were waited for; matrix products, arithmetic and copies ran while one was open for 27% of the time, Pallas kernels for 0%

profile of v1, /device:TPU:0, one launch (start us, length us, event | category | flops | bytes accessed | tf_op | source)
XLA Modules:
  0.0 622.1 jit_solution(12924808723991642465)
XLA Ops:
  9.1 9.8 %copy.81 = bf16[1,16,12288]{1,0,2:T(2,128)(2,1)} copy(bf16[1,16,12288]{2,1,0:T(8,128)(2,1)S(1)} %convert_bitcast_fusion) | data formatting | bytes 786432 | tf_op jit(solution)/shard_map/broadcast_in_dim | solution.py:117
  19.4 67.0 %reduce.7 = bf16[12288,16]{1,0:T(8,128)(2,1)S(1)} reduce(bf16[12288,1,16]{2,1,0:T(2,128)(2,1)} %bitcast.203, bf16[]{:T(256)} %broadcast.313), dimensions={1}, to_apply=%bitcast.148.reduce_sub_computation | reduce | bytes 786434
  86.4 3.9 reshape.466
  90.3 8.1 %all-to-all-start = ((bf16[8,2,12288]{2,1,0:T(2,128)(2,1)}), bf16[8,2,12288]{2,1,0:T(2,128)(2,1)S(1)}, u32[]{:S(2)}, u32[]{:S(2)}) async-start(bf16[8,2,12288]{2,1,0:T(2,128)(2,1)} %reshape.466), calls=%async_computation | async-start | bytes 786432 | tf_op jit(solution)/shard_map/all_to_all | solution.py:116
  99.0 9.2 %all-to-all-done = bf16[8,2,12288]{2,1,0:T(2,128)(2,1)S(1)} async-done(((bf16[8,2,12288]{2,1,0:T(2,128)(2,1)}), bf16[8,2,12288]{2,1,0:T(2,128)(2,1)S(1)}, u32[]{:S(2)}, u32[]{:S(2)}) %all-to-all-start) | async-done | bytes 393248 | tf_op jit(solution)/shard_map/all_to_all | solution.py:116
  108.3 3.4 all-to-all-start.2
  111.6 6.2 %reshape.467 = bf16[12288,1,16]{2,1,0:T(2,128)(2,1)} reshape(bf16[8,2,12288]{2,1,0:T(2,128)(2,1)S(1)} %all-to-all-done) | data formatting | bytes 786432
  117.9 11.4 %copy.82 = bf16[1,16,12288]{2,1,0:T(8,128)(2,1)S(1)} copy(bf16[1,16,12288]{1,0,2:T(2,128)(2,1)} %bitcast.204) | data formatting | bytes 786432 | tf_op jit(solution)/shard_map/all_to_all | solution.py:116
  129.6 3.2 stack.3
  132.9 4.6 all-to-all-start.1
  139.0 3.1 fusion.45
  142.1 97.8 %all-to-all-done.1 = bf16[16,128,1536]{2,1,0:T(8,128)(2,1)} async-done(((bf16[16,128,1536]{2,1,0:T(8,128)(2,1)}), bf16[16,128,1536]{2,1,0:T(8,128)(2,1)}, u32[]{:S(2)}, u32[]{:S(2)}) %all-to-all-start.1) | async-done | bytes 6291488 | tf_op jit(solution)/shard_map/all_to_all | solution.py:18
  239.9 10.5 %fusion.52 = bf16[1024,1536]{1,0:T(8,128)(2,1)S(1)} fusion(bf16[2048,1536]{1,0:T(8,128)(2,1)} %bitcast.3, bf16[1024,2048]{1,0:T(8,128)(2,1)} %all-gather.6.cloned.1.call-done, f32[1024]{0:T(1024)S(1)} %add_rsqrt_fusion.1), kind=kOutput, calls=%fused_computation.65 | convolution fusion | flops 6450315264 | bytes 13635584 | tf_op jit(solution)/shard_map/dot_general | solution.py:136
  252.4 18.8 %while.17 = (s32[]{:T(128)}, f32[2,1,256,512]{3,2,0,1:T(8,128)S(1)}, f32[2,1,256]{2,1,0:T(1,128)S(1)}, f32[2,2,256,1,512]{4,2,0,1,3:T(8,128)}, f32[1]{0:T(128)},...) while((s32[]{:T(128)}, ...), condition=%wide.region_4.5_spmd.clone.clone.clone, body=%wide.region_1.4_spmd.clone.clone.clone.sunk | while | flops 1816989184 | bytes 22576332 | solution.py:97
  259.7 2.0 fusion.98
  269.1 2.0 fusion.98
  274.0 2.1 fusion.67
  276.1 6.0 convolution_convert_fusion.1
  283.2 2.7 copy.89
  285.9 2.2 reshape.464
  288.1 19.3 %all_to_all.79 = bf16[8,2,8192]{2,1,0:T(2,128)(2,1)S(1)} all-to-all(bf16[8,2,8192]{2,1,0:T(2,128)(2,1)S(1)} %reshape.464), channel_id=1, replica_groups=mesh['row'=16,'col'=8] {'col'}, dimensions={0} | all-to-all | bytes 524288 | tf_op jit(solution)/shard_map/all_to_all | solution.py:119
  308.8 3.3 copy.90
  312.1 60.2 %reduce-scatter.3.cloned.1.call-done = bf16[1024,256]{1,0:T(8,128)(2,1)} async-done(((bf16[1024,2048]{1,0:T(8,128)(2,1)}), bf16[1024,256]{1,0:T(8,128)(2,1)}) %reduce-scatter.3.cloned.1.call-update) | async-done | bytes 524304 | tf_op jit(solution)/shard_map/reduce_scatter | solution.py:155
  373.6 21.3 %psum.7 = f32[1024]{0:T(1024)S(1)} all-reduce(f32[1024]{0:T(1024)S(1)} %multiply_reduce_fusion), channel_id=1, replica_groups=mesh['row'=16,'col'=8] {'col'}, use_global_device_ids=true, to_apply=%region_9.10 | all-reduce | flops 1024 | bytes 8192 | tf_op jit(solution)/shard_map/psum | solution.py:158
  395.0 2.1 multiply_convert_fusion
  397.2 13.0 %all_to_all.80 = bf16[8,512,16]{1,2,0:T(8,128)(2,1)} all-to-all(bf16[8,512,16]{1,2,0:T(8,128)(2,1)S(1)} %bitcast.228), channel_id=1, replica_groups=mesh['row'=16,'col'=8] {'col'}, dimensions={0} | all-to-all | bytes 262144 | tf_op jit(solution)/shard_map/all_to_all | solution.py:129
  411.0 76.5 %all-gather.10.cloned.1.call-done = bf16[1024,2048]{1,0:T(8,128)(2,1)} async-done(((bf16[1024,256]{1,0:T(8,128)(2,1)}), bf16[1024,2048]{1,0:T(8,128)(2,1)}) %all-gather.10.cloned.1.call-update) | async-done | bytes 4194320 | tf_op jit(solution)/shard_map/all_gather | solution.py:160
  487.5 9.9 %fusion.55 = f32[2,1024,512]{2,1,0:T(8,128)} fusion(bf16[2,2048,512]{2,1,0:T(8,128)(2,1)} %all-gather.12.cloned.1.call-done, bf16[1024,2048]{1,0:T(8,128)(2,1)} %all-gather.10.cloned.1.call-done), kind=kOutput, calls=%fused_computation.70 | convolution fusion | flops 4294967296 | bytes 12582912 | tf_op jit(solution)/shard_map/td,gdf->gtf/dot_general | solution.py:162
  497.4 23.5 %all-gather.14.cloned.1.call-done = bf16[512,2048]{0,1:T(8,128)(2,1)} async-done(((bf16[512,128]{0,1:T(8,128)(2,1)}), bf16[512,2048]{0,1:T(8,128)(2,1)}) %all-gather.14.cloned.1.call-update) | async-done | bytes 2097168 | tf_op jit(solution)/shard_map/all_gather | solution.py:171
  520.9 7.2 %convolution_convert_fusion = bf16[1024,2048]{1,0:T(8,128)(2,1)} fusion(bf16[512,2048]{0,1:T(8,128)(2,1)} %all-gather.14.cloned.1.call-done, f32[2,1024,512]{2,1,0:T(8,128)} %fusion.55), kind=kOutput, calls=%fused_computation.66 | convolution fusion | flops 2152726528 | bytes 10485760 | tf_op jit(solution)/shard_map/dot_general | solution.py:169
  530.6 82.6 %reduce-scatter.5.cloned.1.call-done = bf16[1024,256]{1,0:T(8,128)(2,1)} async-done(((bf16[1024,2048]{1,0:T(8,128)(2,1)}), bf16[1024,256]{1,0:T(8,128)(2,1)}) %reduce-scatter.5.cloned.1.call-update) | async-done | bytes 524304 | tf_op jit(solution)/shard_map/reduce_scatter | solution.py:174
  613.1 2.1 select_convert_fusion
  (107 shorter events, 31.3 us)
Async XLA Ops:
  7.2 131.8 %all-gather.6.cloned.1.call-start = ((), (), s32[]{:S(2)}) async-start(), calls=%async_computation.7 | async-start | bytes 4718592 | tf_op jit(solution)/shard_map/all_gather | solution.py:133
  86.3 12.0 %copy-start.11 = (f32[4096,16]{0,1:T(8,128)S(1)}, f32[4096,16]{0,1:T(8,128)}, u32[]{:S(2)}) copy-start(f32[4096,16]{0,1:T(8,128)} %param.12) | copy-start | bytes 786436
  90.3 18.0 %all-to-all-start = ((bf16[8,2,12288]{2,1,0:T(2,128)(2,1)}), bf16[8,2,12288]{2,1,0:T(2,128)(2,1)S(1)}, u32[]{:S(2)}, u32[]{:S(2)}) async-start(bf16[8,2,12288]{2,1,0:T(2,128)(2,1)} %reshape.466), calls=%async_computation | async-start | bytes 786432 | tf_op jit(solution)/shard_map/all_to_all | solution.py:116
  108.3 21.3 %all-to-all-start.2 = ((bf16[8,512,16]{1,2,0:T(8,128)(2,1)}), bf16[8,512,16]{1,2,0:T(8,128)(2,1)S(1)}, u32[]{:S(2)}, u32[]{:S(2)}) async-start(bf16[8,512,16]{1,2,0:T(8,128)(2,1)} %bitcast.161), calls=%async_computation.2 | async-start | bytes 262144 | tf_op jit(solution)/shard_map/all_to_all | solution.py:126
  129.6 3.3 copy-start.6
  129.6 3.2 copy-start.7
  132.9 107.0 %all-to-all-start.1 = ((bf16[16,128,1536]{2,1,0:T(8,128)(2,1)}), bf16[16,128,1536]{2,1,0:T(8,128)(2,1)}, u32[]{:S(2)}, u32[]{:S(2)}) async-start(bf16[16,128,1536]{2,1,0:T(8,128)(2,1)} %stack.3), calls=%async_computation.1 | async-start | bytes 12582912 | tf_op jit(solution)/shard_map/all_to_all | solution.py:18
  137.5 138.6 %all-gather.8.cloned.1.call-start = ((), (), s32[]{:S(2)}) async-start(), calls=%async_computation.8 | async-start | bytes 2228224 | tf_op jit(solution)/shard_map/all_gather | solution.py:152
  138.7 233.6 %reduce-scatter.3.cloned.1.call-start = ((), (), s32[]{:S(2)}) async-start(), calls=%async_computation.9 | async-start | bytes 4718592 | tf_op jit(solution)/shard_map/reduce_scatter | solution.py:155
  250.4 1.6 copy-start.5
  252.4 3.3 copy-start.1
  259.7 2.1 copy-start.2
  261.9 3.3 copy-start.1
  269.1 2.1 copy-start.2
  271.3 2.2 copy-start
  282.1 1.0 copy-start.10
  282.1 128.9 %all-gather.12.cloned.1.call-start = ((), (), s32[]{:S(2)}) async-start(), calls=%async_computation.11 | async-start | bytes 4456448 | tf_op jit(solution)/shard_map/all_gather | solution.py:165
  307.4 65.0 %copy-start.3 = (bf16[1024,256]{1,0:T(8,128)(2,1)S(1)}, bf16[1024,256]{1,0:T(8,128)(2,1)}, u32[]{:S(2)}) copy-start(bf16[1024,256]{1,0:T(8,128)(2,1)} %param.8) | copy-start | bytes 1572868
  312.1 85.1 %copy-start.12 = (f32[4096,16]{0,1:T(8,128)S(1)}, f32[4096,16]{0,1:T(8,128)}, u32[]{:S(2)}) copy-start(f32[4096,16]{0,1:T(8,128)} %param.13) | copy-start | bytes 786436
  312.1 175.4 %all-gather.10.cloned.1.call-start = ((), (), s32[]{:S(2)}) async-start(), calls=%async_computation.10 | async-start | bytes 4718592 | tf_op jit(solution)/shard_map/all_gather | solution.py:160
  397.1 123.9 %all-gather.14.cloned.1.call-start = ((), (), s32[]{:S(2)}) async-start(), calls=%async_computation.12 | async-start | bytes 2228224 | tf_op jit(solution)/shard_map/all_gather | solution.py:171
  410.2 203.0 %reduce-scatter.5.cloned.1.call-start = ((), (), s32[]{:S(2)}) async-start(), calls=%async_computation.13 | async-start | bytes 4718592 | tf_op jit(solution)/shard_map/reduce_scatter | solution.py:174
  528.1 0.7 copy-start.13
  528.1 0.9 copy-start.8
  528.1 1.7 copy-start.9
  528.1 85.0 %copy-start.4 = (bf16[1024,256]{1,0:T(8,128)(2,1)S(1)}, bf16[1024,256]{1,0:T(8,128)(2,1)}, u32[]{:S(2)}) copy-start(bf16[1024,256]{1,0:T(8,128)(2,1)} %reduce-scatter.3.cloned.1.call-done) | copy-start | bytes 1572868
Sparse Core Ops, SparseCore 0:
  10.2 76.3 all-gather.5
  140.6 92.9 all-gather.7
  282.2 90.0 reduce-scatter.2
  374.5 36.4 all-gather.11
  413.9 73.5 all-gather.9
  489.2 31.7 all-gather.13
  528.3 84.7 reduce-scatter.4
